TPU v7x, 256 devices: a whole 4x4x8 slice. The times are simulated.
256 devices in a mesh: dp: 8 (over y, core), space: 32 (over z, x).
Axes of the slice: x: 4, y: 4, z: 8, core: 2. Of those that a mesh axis runs over, the one named last changes fastest.
Arguments:
- features: bfloat16 [8, 64, 64, 256], P('dp', None, 'space'), may hold values from -6 to 6
- kernel_a: bfloat16 [27, 64, 128], replicated, may hold values from -0.15625 to 0.15625
- kernel_b: bfloat16 [27, 128, 256], replicated, may hold values from -0.109375 to 0.109375
- upstream: bfloat16 [8, 256, 32, 64], P('dp', None, 'space'), may hold values from -24 to 24
Outputs:
- grad_input: bfloat16 [8, 64, 64, 256], P('dp', None, 'space')
- grad_kernel_a: float32 [27, 64, 128], replicated
- grad_kernel_b: float32 [27, 128, 256], P(None, None, 'space')
All inputs are finite; a program needn't handle non-finite values.
Results may differ from a plain program's by a relative error of at most 0.0075.
Values may be sent and summed in bfloat16 or wider, within the bound.
A program may use at most 64 MiB of HBM per device.

v0:
```python
import math

import jax
import jax.numpy as jnp
from jax import lax
from jax.sharding import PartitionSpec as P

GY = 16
GZ = 16


def with_halo(value, sides, width):
    for axis, dim in sides:
        count, length = (lax.axis_size(axis), value.shape[dim])
        up = [(i, (i + 1) % count) for i in range(count - 1)]
        down = [(j, i) for i, j in up]
        last = lax.slice_in_dim(value, length - width, length, axis=dim)
        leading = lax.slice_in_dim(value, 0, width, axis=dim)
        before = lax.ppermute(last, axis, up)
        after = lax.ppermute(leading, axis, down)
        value = jnp.concatenate([before, value, after], axis=dim)
    return value


def tap_view(padded_flat, off_x, off_y, off_z, planes, span_z, cell_count, column):
    shift_z = off_z - 1
    keep_mask = ((column + shift_z >= 0) & (column + shift_z < span_z)).astype(padded_flat.dtype)
    begin = off_y * span_z + off_z
    return padded_flat[:, :, off_x : off_x + planes, begin : begin + cell_count] * keep_mask


def pad_cells(source, span_z):
    return jnp.pad(source, ((0, 0), (0, 0), (0, 0), (span_z + 1, span_z + 1)))


def pad_planes(source):
    return jnp.pad(source, ((0, 0), (0, 0), (1, 1), (0, 0)))


def conv_forward(rimmed, kernel, planes, span_y, span_z):
    cell_count = span_y * span_z
    padded_flat = pad_cells(rimmed, span_z)
    column = lax.broadcasted_iota(jnp.int32, (cell_count,), 0) % span_z
    summed = None
    for tap_index in range(27):
        shifted = tap_view(
            padded_flat,
            tap_index // 9,
            tap_index // 3 % 3,
            tap_index % 3,
            planes,
            span_z,
            cell_count,
            column,
        )
        product = jnp.einsum(
            "io,sixn->soxn", kernel[tap_index], shifted, preferred_element_type=jnp.float32
        )
        summed = product if summed is None else summed + product
    return summed


def conv_transposed(rimmed, kernel, planes, span_y, span_z):
    cell_count = span_y * span_z
    padded_flat = pad_cells(rimmed, span_z)
    column = lax.broadcasted_iota(jnp.int32, (cell_count,), 0) % span_z
    summed = None
    for tap_index in range(27):
        shifted = tap_view(
            padded_flat,
            2 - tap_index // 9,
            2 - tap_index // 3 % 3,
            2 - tap_index % 3,
            planes,
            span_z,
            cell_count,
            column,
        )
        product = jnp.einsum(
            "io,soxn->sixn", kernel[tap_index], shifted, preferred_element_type=jnp.float32
        )
        summed = product if summed is None else summed + product
    return summed


def kernel_grad(rimmed, gradient, planes, span_y, span_z):
    cell_count = span_y * span_z
    padded_flat = pad_cells(rimmed, span_z)
    column = lax.broadcasted_iota(jnp.int32, (cell_count,), 0) % span_z
    terms = []
    for tap_index in range(27):
        shifted = tap_view(
            padded_flat,
            tap_index // 9,
            tap_index // 3 % 3,
            tap_index % 3,
            planes,
            span_z,
            cell_count,
            column,
        )
        terms.append(
            jnp.einsum("sixn,soxn->io", shifted, gradient, preferred_element_type=jnp.float32)
        )
    return jnp.stack(terms)


def silu_slope(value):
    sigma = jax.nn.sigmoid(value)
    return sigma * (1.0 + value * (1.0 - sigma))


def body(features, kernel_a, kernel_b, upstream):
    samples = features.shape[0]
    planes = features.shape[2]
    half_planes = planes // 2
    half_y, half_z = (GY // 2, GZ // 2)
    rimmed_in = with_halo(features, (("space", 2),), 1)
    pre_a = conv_forward(rimmed_in, kernel_a, planes, GY, GZ)
    filters_a = pre_a.shape[1]
    pooled = (
        jax.nn.silu(pre_a)
        .reshape(samples, filters_a, half_planes, 2, half_y, 2, half_z, 2)
        .mean(axis=(3, 5, 7))
    )
    pooled = pooled.reshape(samples, filters_a, half_planes, half_y * half_z).astype(jnp.bfloat16)
    per_device = kernel_b.shape[2] // lax.axis_size("space")
    gathered = lax.all_gather(pooled, "space", axis=2, tiled=True)
    full_planes = gathered.shape[2]
    own_kernel = lax.dynamic_slice_in_dim(
        kernel_b, lax.axis_index("space") * per_device, per_device, 2
    )
    padded_pooled = pad_planes(gathered)
    pre_b = conv_forward(padded_pooled, own_kernel, full_planes, half_y, half_z)
    upstream_own = lax.all_to_all(upstream, "space", split_axis=1, concat_axis=2, tiled=True)
    grad_pre_b = (upstream_own.astype(jnp.float32) * silu_slope(pre_b)).astype(jnp.bfloat16)
    part_b = kernel_grad(padded_pooled, grad_pre_b, full_planes, half_y, half_z)
    padded_grad = pad_planes(grad_pre_b)
    term_rows = conv_transposed(
        padded_grad, own_kernel, half_planes * lax.axis_size("space"), half_y, half_z
    )
    own_rows = lax.psum_scatter(
        jnp.transpose(term_rows, (2, 0, 1, 3)), "space", scatter_dimension=0, tiled=True
    )
    grad_pool = jnp.transpose(own_rows, (1, 2, 0, 3))
    samples_all = samples * lax.axis_size("dp")
    cells_all = planes * lax.axis_size("space") * GY * GZ
    scale_a = 1.0 / math.sqrt(samples_all * cells_all)
    scale_b = 1.0 / math.sqrt(samples_all * cells_all / 8)
    grad_kernel_b = lax.psum(part_b, "dp") * scale_b
    spread = jnp.broadcast_to(
        grad_pool.reshape(samples, filters_a, half_planes, 1, half_y, 1, half_z, 1),
        (samples, filters_a, half_planes, 2, half_y, 2, half_z, 2),
    )
    spread = spread.reshape(samples, filters_a, planes, GY * GZ)
    grad_pre_a = (spread * 0.125 * silu_slope(pre_a)).astype(jnp.bfloat16)
    part_a = kernel_grad(rimmed_in, grad_pre_a, planes, GY, GZ)
    grad_kernel_a = lax.psum(part_a, ("dp", "space")) * scale_a
    rimmed_back = with_halo(grad_pre_a, (("space", 2),), 1)
    grad_input = conv_transposed(rimmed_back, kernel_a, planes, GY, GZ).astype(jnp.bfloat16)
    return (grad_input, grad_kernel_a, grad_kernel_b)


def solution(mesh):
    return jax.shard_map(
        body,
        mesh=mesh,
        in_specs=(P("dp", None, "space", None), P(), P(), P("dp", None, "space", None)),
        out_specs=(P("dp", None, "space", None), P(), P(None, None, "space")),
        check_vma=False,
    )
```

profile of v0, /device:TPU:1, one launch (start us, length us, event | category | flops | bytes accessed | tf_op | source)
XLA Modules:
  0.0 672.9 jit_solution(3354463360023690337)
XLA Ops:
  9.1 3.9 collective-permute-start
  17.5 12.8 %all-to-all-start = ((bf16[32,2,256]{2,1,0:T(2,128)(2,1)}), bf16[32,2,256]{2,1,0:T(2,128)(2,1)S(1)}, u32[]{:S(2)}, u32[]{:S(2)}) async-start(bf16[32,2,256]{2,1,0:T(2,128)(2,1)} %reshape.962), calls=%async_computation | async-start | bytes 65536 | tf_op jit(solution)/shard_map/all_to_all | solution.py:135
  30.5 1.5 select_maximum_fusion
  33.1 1.5 fusion.371
  42.4 38.8 %all_gather.3 = bf16[1,128,32,64]{1,3,0,2:T(8,128)(2,1)S(1)} all-gather(bf16[1,128,1,64]{1,3,0,2:T(8,128)(2,1)S(1)} %fusion.606), channel_id=1, replica_groups=mesh['dp'=8,'space'=32] {'space'}, dimensions={2}, use_global_device_ids=true | all-gather | bytes 540672 | tf_op jit(solution)/shard_map/all_gather | solution.py:128
  102.7 1.9 multiply_convert_fusion.1
  105.6 1.7 fusion.440
  107.9 1.7 convolution_bitcast_fusion.2
  109.6 1.6 convolution_bitcast_fusion.5
  111.2 1.6 convolution_bitcast_fusion.7
  112.9 1.6 convolution_bitcast_fusion.8
  114.5 1.7 convolution_bitcast_fusion.3
  116.2 1.9 convolution_bitcast_fusion.6
  118.1 1.6 convolution_bitcast_fusion.9
  119.7 1.7 convolution_bitcast_fusion
  145.9 1.9 convolution_add_fusion.14
  157.9 2.1 fusion.12
  160.0 60.2 %all-reduce.11.cloned.1.call-done = f32[27,128,8]{1,2,0:T(8,128)} async-done(((f32[27,128,8]{1,2,0:T(8,128)}), f32[27,128,8]{1,2,0:T(8,128)}) %all-reduce.11.cloned.1.call-update) | async-done | bytes 110608 | tf_op jit(solution)/shard_map/psum | solution.py:150
  220.2 1.6 broadcast_multiply_fusion.1
  221.8 161.0 %reduce-scatter.2.cloned.1.call-done = f32[1,1,128,64]{2,3,0,1:T(8,128)} async-done(((f32[32,1,128,64]{2,3,0,1:T(8,128)}), f32[1,1,128,64]{2,3,0,1:T(8,128)}) %reduce-scatter.2.cloned.1.call-update) | async-done | bytes 32784 | tf_op jit(solution)/shard_map/reduce_scatter | solution.py:142
  393.9 2.2 collective-permute-start.2
  398.5 2.8 collective-permute-done.3
  408.7 254.2 %all-reduce.9.cloned.1.call-done = f32[27,64,128]{2,1,0:T(8,128)} async-done(((f32[27,64,128]{2,1,0:T(8,128)}), f32[27,64,128]{2,1,0:T(8,128)}) %all-reduce.9.cloned.1.call-update) | async-done | bytes 884752 | tf_op jit(solution)/shard_map/psum | solution.py:158
  662.9 2.2 broadcast_multiply_fusion
  (323 shorter events, 91.8 us)
Async XLA Ops:
  8.0 73.2 %copy-start = (bf16[27,128,256]{2,1,0:T(8,128)(2,1)S(1)}, bf16[27,128,256]{2,1,0:T(8,128)(2,1)}, u32[]{:S(2)}) copy-start(bf16[27,128,256]{2,1,0:T(8,128)(2,1)} %param.6) | copy-start | bytes 5308420
  9.1 21.3 %collective-permute-start = (bf16[1,64,1,256]{3,2,1,0:T(2,128)(2,1)S(1)}, bf16[1,64,1,256]{3,2,1,0:T(2,128)(2,1)S(1)}, u32[]{:S(2)}, u32[]{:S(2)}) collective-permute-start(bf16[1,64,1,256]{3,2,1,0:T(2,128)(2,1)S(1)} %get-tuple-element.50), channel_id=1, source_target_pairs={{0,1},{1,2},{2,3},{3,4},{4,5},{5,6},{6,7},{7,8},{8,9},{9,10},{10,1... | collective-permute-start | bytes 98312 | tf_op jit(solution)/shard_map/ppermute | solution.py:19
  13.1 17.4 %collective-permute-start.1 = (bf16[1,64,1,256]{3,2,1,0:T(2,128)(2,1)S(1)}, bf16[1,64,1,256]{3,2,1,0:T(2,128)(2,1)S(1)}, u32[]{:S(2)}, u32[]{:S(2)}) collective-permute-start(bf16[1,64,1,256]{3,2,1,0:T(2,128)(2,1)S(1)} %get-tuple-element.51), channel_id=1, source_target_pairs={{1,0},{2,1},{3,2},{4,3},{5,4},{6,5},{7,6},{8,7},{9,8},{10,9},{11,1... | collective-permute-start | bytes 98312 | tf_op jit(solution)/shard_map/ppermute | solution.py:20
  17.5 84.9 %all-to-all-start = ((bf16[32,2,256]{2,1,0:T(2,128)(2,1)}), bf16[32,2,256]{2,1,0:T(2,128)(2,1)S(1)}, u32[]{:S(2)}, u32[]{:S(2)}) async-start(bf16[32,2,256]{2,1,0:T(2,128)(2,1)} %reshape.962), calls=%async_computation | async-start | bytes 65536 | tf_op jit(solution)/shard_map/all_to_all | solution.py:135
  30.3 189.9 %all-reduce.11.cloned.1.call-start = ((), (), s32[]{:S(2)}) async-start(), calls=%async_computation.4 | async-start | bytes 221184 | tf_op jit(solution)/shard_map/psum | solution.py:150
  81.2 23.5 %copy-start.10 = (bf16[1,128,34,64]{1,3,0,2:T(8,128)(2,1)}, bf16[1,128,34,64]{1,3,0,2:T(8,128)(2,1)S(1)}, u32[]{:S(2)}) copy-start(bf16[1,128,34,64]{1,3,0,2:T(8,128)(2,1)S(1)} %pad.27) | copy-start | bytes 1671172
  145.8 236.9 %reduce-scatter.2.cloned.1.call-start = ((), (), s32[]{:S(2)}) async-start(), calls=%async_computation.2 | async-start | bytes 1081344 | tf_op jit(solution)/shard_map/reduce_scatter | solution.py:142
  157.9 225.7 %copy-start.12 = (f32[1,128,2,256]{1,3,2,0:T(8,128)S(1)}, f32[1,128,2,256]{1,3,2,0:T(8,128)}, u32[]{:S(2)}) copy-start(f32[1,128,2,256]{1,3,2,0:T(8,128)} %get-tuple-element.53) | copy-start | bytes 786436
  159.9 226.4 %copy-start.34 = (bf16[64,2,256]{2,1,0:T(2,128)(2,1)S(1)}, bf16[64,2,256]{2,1,0:T(2,128)(2,1)}, u32[]{:S(2)}) copy-start(bf16[64,2,256]{2,1,0:T(2,128)(2,1)} %copy-done.33) | copy-start | bytes 196612
  159.9 228.7 %copy-start.28 = (bf16[64,2,256]{2,1,0:T(2,128)(2,1)S(1)}, bf16[64,2,256]{2,1,0:T(2,128)(2,1)}, u32[]{:S(2)}) copy-start(bf16[64,2,256]{2,1,0:T(2,128)(2,1)} %copy-done.27) | copy-start | bytes 196612
  160.0 230.9 %copy-start.24 = (bf16[64,2,256]{2,1,0:T(2,128)(2,1)S(1)}, bf16[64,2,256]{2,1,0:T(2,128)(2,1)}, u32[]{:S(2)}) copy-start(bf16[64,2,256]{2,1,0:T(2,128)(2,1)} %copy-done.23) | copy-start | bytes 196612
  160.0 231.1 %copy-start.32 = (bf16[64,2,256]{2,1,0:T(2,128)(2,1)S(1)}, bf16[64,2,256]{2,1,0:T(2,128)(2,1)}, u32[]{:S(2)}) copy-start(bf16[64,2,256]{2,1,0:T(2,128)(2,1)} %copy-done.31) | copy-start | bytes 196612
  160.0 231.2 %copy-start.30 = (bf16[64,2,256]{2,1,0:T(2,128)(2,1)S(1)}, bf16[64,2,256]{2,1,0:T(2,128)(2,1)}, u32[]{:S(2)}) copy-start(bf16[64,2,256]{2,1,0:T(2,128)(2,1)} %copy-done.29) | copy-start | bytes 196612
  160.0 502.9 %all-reduce.9.cloned.1.call-start = ((), (), s32[]{:S(2)}) async-start(), calls=%async_computation.3 | async-start | bytes 1769472 | tf_op jit(solution)/shard_map/psum | solution.py:158
  221.8 169.6 %copy-start.18 = (bf16[64,2,256]{2,1,0:T(2,128)(2,1)S(1)}, bf16[64,2,256]{2,1,0:T(2,128)(2,1)}, u32[]{:S(2)}) copy-start(bf16[64,2,256]{2,1,0:T(2,128)(2,1)} %copy-done.17) | copy-start | bytes 196612
  383.5 8.0 %copy-start.26 = (bf16[64,2,256]{2,1,0:T(2,128)(2,1)S(1)}, bf16[64,2,256]{2,1,0:T(2,128)(2,1)}, u32[]{:S(2)}) copy-start(bf16[64,2,256]{2,1,0:T(2,128)(2,1)} %copy-done.25) | copy-start | bytes 196612
  383.6 8.2 %copy-start.58 = (bf16[64,2,256]{2,1,0:T(2,128)(2,1)S(1)}, bf16[64,2,256]{2,1,0:T(2,128)(2,1)}, u32[]{:S(2)}) copy-start(bf16[64,2,256]{2,1,0:T(2,128)(2,1)} %copy-done.57) | copy-start | bytes 196612
  384.7 7.4 %copy-start.22 = (bf16[64,2,256]{2,1,0:T(2,128)(2,1)S(1)}, bf16[64,2,256]{2,1,0:T(2,128)(2,1)}, u32[]{:S(2)}) copy-start(bf16[64,2,256]{2,1,0:T(2,128)(2,1)} %copy-done.21) | copy-start | bytes 196612
  392.5 8.8 %copy-start.16 = (bf16[27,64,128]{2,1,0:T(8,128)(2,1)S(1)}, bf16[27,64,128]{2,1,0:T(8,128)(2,1)}, u32[]{:S(2)}) copy-start(bf16[27,64,128]{2,1,0:T(8,128)(2,1)} %param.5) | copy-start | bytes 1327108
  392.5 8.8 %copy-start.68 = (bf16[256]{0:T(256)(128)(2,1)S(1)}, bf16[256]{0:T(256)(128)(2,1)}, u32[]{:S(2)}) copy-start(bf16[256]{0:T(256)(128)(2,1)} %copy-done.67) | copy-start | bytes 1540
  393.2 8.7 %copy-start.64 = (bf16[256]{0:T(256)(128)(2,1)S(1)}, bf16[256]{0:T(256)(128)(2,1)}, u32[]{:S(2)}) copy-start(bf16[256]{0:T(256)(128)(2,1)} %copy-done.63) | copy-start | bytes 1540
  393.7 8.6 %copy-start.66 = (bf16[256]{0:T(256)(128)(2,1)S(1)}, bf16[256]{0:T(256)(128)(2,1)}, u32[]{:S(2)}) copy-start(bf16[256]{0:T(256)(128)(2,1)} %copy-done.65) | copy-start | bytes 1540
  393.9 4.6 collective-permute-start.2
  396.1 5.2 collective-permute-start.3
  (53 other events, 201.4 us)
Sparse Core Ops, SparseCore 0:
  146.0 74.2 all-reduce.10
Sparse Core Ops, SparseCore 1:
  160.0 222.6 reduce-scatter.1
  398.6 264.3 all-reduce.8
where the time goes:
time: 680 us; the launch traced here: 673 us
  waiting for transfers between devices  478 us (70%)
  matrix products  99.3 us (15%)
  blocking collectives  38.8 us (6%)
  starting transfers between devices  21.6 us (3%)
  between operations  17.5 us (3%)
  other arithmetic  10.4 us (2%)
  local copies, waits for them, and re-layouts  7.13 us (1%)
    psum x1, waiting for transfers between devices, body(): grad_kernel_a = lax.psum(part_a, ('dp', 'space')) * scale_a  254 us
    reduce_scatter x1, waiting for transfers between devices, body(): lax.psum_scatter(jnp.transpose(term_rows, (2, 0, 1, 3)), 'space', scatter...  161 us
    psum x1, waiting for transfers between devices, body(): grad_kernel_b = lax.psum(part_b, 'dp') * scale_b  60.2 us
    all_gather x1, blocking collectives, body(): gathered = lax.all_gather(pooled, 'space', axis=2, tiled=True)  38.8 us
    dot_general x54, matrix products, conv_transposed(): jnp.einsum('io,soxn->sixn', kernel[tap_index], shifted, preferred_element...  36.3 us
    dot_general x54, matrix products, kernel_grad(): jnp.einsum('sixn,soxn->io', shifted, gradient, preferred_element_type=jnp...  33.3 us
    dot_general x54, matrix products, conv_forward(): jnp.einsum('io,sixn->soxn', kernel[tap_index], shifted, preferred_element...  29.7 us
  transfers between devices with their start and end apart: 8, of which 4 were waited for; matrix products, arithmetic and copies ran while one was open for 8% of the time, Pallas kernels for 0%

commit v1 on v0

v1 whole, which is shorter than its diff:
```python
import functools
import math

import jax
import jax.numpy as jnp
from jax import lax
from jax.experimental import pallas as pl
from jax.experimental.pallas import tpu as pltpu
from jax.sharding import PartitionSpec as P

GY = 16
GZ = 16
CELLS = GY * GZ
HY = GY // 2
HZ = GZ // 2
POOL = HY * HZ
MESH = pl.DeviceIdType.MESH
F32 = jnp.float32
BF16 = jnp.bfloat16

X_R, X_L, P_R, P_L, G_R, G_L, A_R, A_L, DP_P, DP_G, A1, A2, A3, A4, B2, B3, N_SEM = range(17)


def sigmoid(value):
    return 1.0 / (1.0 + jnp.exp(-value))


def slope(value, sigma):
    return sigma * (1.0 + value * (1.0 - sigma))


def shift_column(value, step, span):
    if step == 0:
        return value
    rows = value.shape[0]
    column = lax.broadcasted_iota(jnp.int32, value.shape, 0) % span + step
    moved = pltpu.roll(value, (-step) % rows, 0)
    return jnp.where((column >= 0) & (column < span), moved, 0.0)


def shift_block(value, step):
    if step == 0:
        return value
    zeros = jnp.zeros((abs(step), value.shape[1]), value.dtype)
    if step > 0:
        return jnp.concatenate([value[step:], zeros], axis=0)
    return jnp.concatenate([zeros, value[:step]], axis=0)


def kernel(
    nd, ns, scale_a, scale_b,
    x_ref, wa_ref, wb_ref, up_ref,
    gi_ref, ga_ref, gb_ref,
    xh, xz, slope_a, act_a, pown, ph, gbown, gbh, gaown, gah, gz, kr, spread,
    psend, precv, grecv, pcol, a1send, a1recv, a2send, a2recv, a3buf, a4buf,
    bsend, brecv, bag, send, recv,
):
    s = lax.axis_index("space")
    d = lax.axis_index("dp")
    right = lax.rem(s + 1, ns)
    left = lax.rem(s + ns - 1, ns)
    has_left = s > 0
    has_right = s < ns - 1

    barrier = pltpu.get_barrier_semaphore()

    def greet_space(k, c):
        pl.semaphore_signal(barrier, inc=1, device_id={"space": lax.rem(s + k, ns)}, device_id_type=MESH)
        return c

    def greet_dp(k, c):
        pl.semaphore_signal(barrier, inc=1, device_id={"dp": lax.rem(d + k, nd)}, device_id_type=MESH)
        return c

    lax.fori_loop(1, ns, greet_space, 0)
    lax.fori_loop(1, nd, greet_dp, 0)

    for t in range(9):
        for j in range(3):
            kr[t, :, j * 128 : (j + 1) * 128] = wa_ref[t, j * 64 : (j + 1) * 64, :]
    for q in range(4):
        xz[q, 0:GZ, :] = jnp.zeros((GZ, 192), BF16)
        xz[q, GZ + CELLS : 2 * GZ + CELLS, :] = jnp.zeros((GZ, 192), BF16)
        gz[q, 0:GZ, :] = jnp.zeros((GZ, 384), BF16)
        gz[q, GZ + CELLS : 2 * GZ + CELLS, :] = jnp.zeros((GZ, 384), BF16)

    pl.semaphore_wait(barrier, ns + nd - 2)

    def remote(src, dst, slot, device):
        return pltpu.make_async_remote_copy(
            src_ref=src, dst_ref=dst, send_sem=send.at[slot], recv_sem=recv.at[slot],
            device_id=device, device_id_type=MESH,
        )

    def halo(lower, upper, landing, slot_r, slot_l):
        to_right = remote(upper, landing.at[0], slot_r, {"space": right})
        to_left = remote(lower, landing.at[1], slot_l, {"space": left})
        to_right.start()
        to_left.start()
        return to_right, to_left

    def to_all(axis, me, count, src_of, dst, slot):
        def step(k, c):
            other = lax.rem(me + k, count)
            remote(src_of(other), dst.at[me], slot, {axis: other}).start()
            return c

        lax.fori_loop(1, count, step, 0)

    def wait_all(sems, slot, buf, count):
        part = buf.at[pl.ds(0, count - 1)]
        pltpu.make_async_copy(part, part, sems.at[slot]).wait()

    x_halo = halo(x_ref.at[0], x_ref.at[1], xh, X_R, X_L)

    def put_xz(q, plane):
        rows = plane.astype(F32).T
        wide = jnp.concatenate([shift_column(rows, -1, GZ), rows, shift_column(rows, 1, GZ)], axis=1)
        xz[q, GZ : GZ + CELLS, :] = wide.astype(BF16)

    put_xz(1, x_ref[0])
    put_xz(2, x_ref[1])

    def conv_a_terms(q, exs):
        total = None
        for ex in exs:
            for ey in range(3):
                part = jnp.dot(
                    xz[q + ex, ey * GZ : ey * GZ + CELLS, :], wa_ref[ex * 3 + ey],
                    preferred_element_type=F32,
                )
                total = part if total is None else total + part
        return total

    act_a[0:CELLS, :] = conv_a_terms(0, (1, 2))
    act_a[CELLS : 2 * CELLS, :] = conv_a_terms(1, (0, 1))
    x_halo[0].wait_recv()
    put_xz(0, jnp.where(has_left, xh[0].astype(F32), 0.0))
    x_halo[1].wait_recv()
    put_xz(3, jnp.where(has_right, xh[1].astype(F32), 0.0))
    for q in range(2):
        area = slice(q * CELLS, (q + 1) * CELLS)
        pre = act_a[area, :] + conv_a_terms(q, (0,) if q == 0 else (2,))
        sigma = sigmoid(pre)
        act_a[area, :] = pre * sigma
        slope_a[area, :] = slope(pre, sigma) * 0.125

    pairs = act_a[pl.ds(0, CELLS, stride=2), :] + act_a[pl.ds(1, CELLS, stride=2), :]
    pairs = pairs.reshape(2, HY, 2, HZ, 128)
    pooled = (pairs[0, :, 0] + pairs[0, :, 1] + pairs[1, :, 0] + pairs[1, :, 1]).reshape(POOL, 128) * 0.125
    pown[...] = pooled.astype(BF16)
    p_halo = halo(pown, pown, ph, P_R, P_L)

    def conv_b_terms(plane, ex):
        taps = []
        moved = [shift_column(plane, step, HZ) for step in (-1, 0, 1)]
        for ey in range(3):
            for ez in range(3):
                taps.append(shift_block(moved[ez], (ey - 1) * HZ).astype(BF16))
        return jnp.dot(jnp.concatenate(taps, axis=1), wb_ref[ex], preferred_element_type=F32)

    own_p = pown[...].astype(F32)
    pre_b = conv_b_terms(own_p, 1)
    p_halo[0].wait_recv()
    left_p = jnp.where(has_left, ph[0].astype(F32), 0.0)
    pre_b = pre_b + conv_b_terms(left_p, 0)
    p_halo[1].wait_recv()
    right_p = jnp.where(has_right, ph[1].astype(F32), 0.0)
    pre_b = pre_b + conv_b_terms(right_p, 2)
    grad_b = up_ref[...].astype(F32) * slope(pre_b, sigmoid(pre_b))
    gbown[...] = grad_b.astype(BF16)
    g_halo = halo(gbown, gbown, gbh, G_R, G_L)

    chans = 128 // nd
    for e, plane in enumerate((left_p, own_p, right_p)):
        psend[:, e] = plane.T.reshape(nd, chans, POOL).astype(BF16)
    grecv[d] = gbown[...]
    precv[d] = psend[d]
    to_all("dp", d, nd, lambda other: psend.at[other], precv, DP_P)
    to_all("dp", d, nd, lambda other: gbown, grecv, DP_G)

    def conv_bt_terms(plane, ex, total):
        moved = [shift_column(plane, -step, HZ) for step in (-1, 0, 1)]
        for ey in range(3):
            for ez in range(3):
                tap = ey * 3 + ez
                shifted = shift_block(moved[ez], -(ey - 1) * HZ).astype(BF16)
                part = lax.dot_general(
                    shifted, wb_ref[ex, tap * 128 : (tap + 1) * 128, :],
                    (((1,), (1,)), ((), ())), preferred_element_type=F32,
                )
                total = part if total is None else total + part
        return total

    grad_pool = conv_bt_terms(gbown[...].astype(F32), 1, None)
    g_halo[0].wait_recv()
    grad_pool = conv_bt_terms(jnp.where(has_left, gbh[0].astype(F32), 0.0), 2, grad_pool)
    g_halo[1].wait_recv()
    grad_pool = conv_bt_terms(jnp.where(has_right, gbh[1].astype(F32), 0.0), 0, grad_pool)

    tall = jnp.broadcast_to(grad_pool.reshape(HY, 1, HZ, 128), (HY, 2, HZ, 128)).reshape(GY * HZ, 128)
    spread[pl.ds(0, GY * HZ, stride=2), :] = tall
    spread[pl.ds(1, GY * HZ, stride=2), :] = tall
    for q in range(2):
        gaown[q] = (spread[...] * slope_a[q * CELLS : (q + 1) * CELLS, :]).astype(BF16)
    a_halo = halo(gaown.at[0], gaown.at[1], gah, A_R, A_L)

    rows_a = 64 // nd
    grads = [gaown[0], gaown[1]]
    for ex in range(3):
        for ey in range(3):
            term = None
            for q in range(2):
                part = lax.dot_general(
                    xz[q + ex, ey * GZ : ey * GZ + CELLS, :], grads[q],
                    (((0,), (0,)), ((), ())), preferred_element_type=F32,
                )
                term = part if term is None else term + part
            for ez in range(3):
                tap = ex * 9 + ey * 3 + ez
                a1send[:, tap] = term[ez * 64 : (ez + 1) * 64, :].reshape(nd, rows_a, 128).astype(BF16)
    taps_own = a2recv.shape[1]
    for tap in range(27, taps_own * ns):
        a1send[:, tap] = jnp.zeros((nd, rows_a, 128), BF16)
    a1recv[d] = a1send[d]
    to_all("dp", d, nd, lambda other: a1send.at[other], a1recv, A1)

    def put_gz(q, plane):
        wide = jnp.concatenate([shift_column(plane, 1, GZ), plane, shift_column(plane, -1, GZ)], axis=1)
        gz[q, GZ : GZ + CELLS, :] = wide.astype(BF16)

    put_gz(1, gaown[0].astype(F32))
    put_gz(2, gaown[1].astype(F32))
    a_halo[0].wait_recv()
    put_gz(0, jnp.where(has_left, gah[0].astype(F32), 0.0))
    a_halo[1].wait_recv()
    put_gz(3, jnp.where(has_right, gah[1].astype(F32), 0.0))
    for q in range(2):
        total = None
        for ex in range(3):
            for ey in range(3):
                part = lax.dot_general(
                    kr[ex * 3 + ey], gz[q + 2 - ex, (2 - ey) * GZ : (2 - ey) * GZ + CELLS, :],
                    (((1,), (1,)), ((), ())), preferred_element_type=F32,
                )
                total = part if total is None else total + part
        gi_ref[q] = total.astype(BF16)

    wait_all(recv, DP_P, precv, nd)
    wait_all(recv, DP_G, grecv, nd)
    wide_cells = nd * POOL
    lane = lax.broadcasted_iota(jnp.int32, (chans, wide_cells), 1)
    row = lane // HZ % HY
    column = lane % HZ
    for ex in range(3):
        flat = jnp.concatenate([precv[n, ex].astype(F32) for n in range(nd)], axis=1)
        for ey in range(3):
            for ez in range(3):
                step = (ey - 1) * HZ + ez - 1
                inside = (row + ey - 1 >= 0) & (row + ey - 1 < HY) & (column + ez - 1 >= 0) & (column + ez - 1 < HZ)
                moved = flat if step == 0 else pltpu.roll(flat, (-step) % wide_cells, 1)
                tap = ex * 9 + ey * 3 + ez
                pcol[tap * chans : (tap + 1) * chans, :] = jnp.where(inside, moved, 0.0).astype(BF16)
    used = 27 * chans
    padded = pcol.shape[0]
    pcol[used:padded, :] = jnp.zeros((padded - used, wide_cells), BF16)
    part_b = jnp.dot(pcol[...], grecv[...].reshape(wide_cells, 256), preferred_element_type=F32)
    bsend[...] = part_b.T.reshape(ns, 256 // ns, padded).astype(BF16)
    brecv[s] = bsend[s]
    to_all("space", s, ns, lambda other: bsend.at[other], brecv, B2)

    wait_all(recv, A1, a1recv, nd)
    total = a1recv[0].astype(F32)
    for n in range(1, nd):
        total = total + a1recv[n].astype(F32)
    a2send[...] = total.astype(BF16).reshape(a2send.shape)
    a2recv[s] = a2send[s]
    to_all("space", s, ns, lambda other: a2send.at[other], a2recv, A2)

    wait_all(recv, B2, brecv, ns)
    total_b = jnp.sum(brecv[...].astype(F32), axis=0) * scale_b
    bag[d] = total_b.astype(BF16)
    to_all("dp", d, nd, lambda other: bag.at[d], bag, B3)

    wait_all(recv, A2, a2recv, ns)
    total_a = jnp.sum(a2recv[...].astype(F32), axis=0) * scale_a
    a3buf[s] = total_a.astype(BF16)
    to_all("space", s, ns, lambda other: a3buf.at[s], a3buf, A3)
    wait_all(recv, A3, a3buf, ns)
    a4buf[d] = a3buf[...]
    to_all("dp", d, nd, lambda other: a3buf, a4buf, A4)
    wait_all(recv, B3, bag, nd)
    gb_ref[...] = bag[...]
    wait_all(recv, A4, a4buf, nd)
    ga_ref[...] = a4buf[...]

    for pair in (x_halo, p_halo, g_halo, a_halo):
        pair[0].wait_send()
        pair[1].wait_send()
    for slot, buf, count in (
        (DP_P, precv, nd), (DP_G, grecv, nd), (A1, a1recv, nd), (A2, a2recv, ns),
        (A3, a3buf, ns), (A4, a4buf, nd), (B2, brecv, ns), (B3, bag, nd),
    ):
        wait_all(send, slot, buf, count)


def body(nd, ns, scale_a, scale_b, features, kernel_a, kernel_b, upstream):
    x = jnp.transpose(features[0], (1, 0, 2))
    wa = kernel_a.reshape(9, 192, 128)
    wb = kernel_b.reshape(3, 9 * 128, 256)
    up = upstream[0, :, 0, :].T
    rows_a = 64 // nd
    chans = 128 // nd
    taps_own = -(-27 // ns)
    padded = -(-27 * chans // 128) * 128
    vmem = pl.BlockSpec(memory_space=pltpu.VMEM)
    gi, ga, gb = pl.pallas_call(
        functools.partial(kernel, nd, ns, scale_a, scale_b),
        out_shape=(
            jax.ShapeDtypeStruct((2, 64, CELLS), BF16),
            jax.ShapeDtypeStruct((nd, ns, taps_own, rows_a, 128), BF16),
            jax.ShapeDtypeStruct((nd, 256 // ns, padded), BF16),
        ),
        in_specs=[vmem] * 4,
        out_specs=(vmem, vmem, vmem),
        scratch_shapes=[
            pltpu.VMEM((2, 64, CELLS), BF16),
            pltpu.VMEM((4, CELLS + 2 * GZ, 192), BF16),
            pltpu.VMEM((2 * CELLS, 128), F32),
            pltpu.VMEM((2 * CELLS, 128), F32),
            pltpu.VMEM((POOL, 128), BF16),
            pltpu.VMEM((2, POOL, 128), BF16),
            pltpu.VMEM((POOL, 256), BF16),
            pltpu.VMEM((2, POOL, 256), BF16),
            pltpu.VMEM((2, CELLS, 128), BF16),
            pltpu.VMEM((2, CELLS, 128), BF16),
            pltpu.VMEM((4, CELLS + 2 * GZ, 384), BF16),
            pltpu.VMEM((9, 64, 384), BF16),
            pltpu.VMEM((CELLS, 128), F32),
            pltpu.VMEM((nd, 3, chans, POOL), BF16),
            pltpu.VMEM((nd, 3, chans, POOL), BF16),
            pltpu.VMEM((nd, POOL, 256), BF16),
            pltpu.VMEM((padded, nd * POOL), BF16),
            pltpu.VMEM((nd, ns * taps_own, rows_a, 128), BF16),
            pltpu.VMEM((nd, ns * taps_own, rows_a, 128), BF16),
            pltpu.VMEM((ns, taps_own, rows_a, 128), BF16),
            pltpu.VMEM((ns, taps_own, rows_a, 128), BF16),
            pltpu.VMEM((ns, taps_own, rows_a, 128), BF16),
            pltpu.VMEM((nd, ns, taps_own, rows_a, 128), BF16),
            pltpu.VMEM((ns, 256 // ns, padded), BF16),
            pltpu.VMEM((ns, 256 // ns, padded), BF16),
            pltpu.VMEM((nd, 256 // ns, padded), BF16),
            pltpu.SemaphoreType.DMA((N_SEM,)),
            pltpu.SemaphoreType.DMA((N_SEM,)),
        ],
        compiler_params=pltpu.CompilerParams(collective_id=0, has_side_effects=True),
    )(x, wa, wb, up)
    grad_input = jnp.transpose(gi, (1, 0, 2))[None]
    ga = ga.reshape(nd, ns * taps_own, rows_a, 128)[:, :27]
    grad_a = jnp.transpose(ga, (1, 0, 2, 3)).reshape(27, 64, 128).astype(F32)
    gb = gb[:, :, : 27 * chans].reshape(nd, 256 // ns, 27, chans)
    grad_b = jnp.transpose(gb, (2, 0, 3, 1)).reshape(27, 128, 256 // ns).astype(F32)
    return grad_input, grad_a, grad_b


def solution(mesh):
    nd, ns = mesh.shape["dp"], mesh.shape["space"]
    cells_all = nd * 2 * ns * CELLS
    run = functools.partial(body, nd, ns, 1.0 / math.sqrt(cells_all), 1.0 / math.sqrt(cells_all / 8))
    return jax.shard_map(
        run,
        mesh=mesh,
        in_specs=(P("dp", None, "space", None), P(), P(), P("dp", None, "space", None)),
        out_specs=(P("dp", None, "space", None), P(), P(None, None, "space")),
        check_vma=False,
    )
```

time: 680 us -> 66 us (0.10); the launches traced: 673 us -> 65.8 us
  waiting for transfers between devices: 478 us -> 0 us
  matrix products: 99.3 us -> 0 us
  Pallas kernels: 0 us -> 59.2 us
  blocking collectives: 38.8 us -> 0 us
  starting transfers between devices: 21.6 us -> 0 us
  between operations: 17.5 us -> 0.67 us
  other arithmetic: 10.4 us -> 1.86 us
    psum x2 -> x0, waiting for transfers between devices: 314 us -> none  [the longest x1 254 us: body(): grad_kernel_a = lax.psum(part_a, ('dp', 'space')) * scale_a]
    reduce_scatter x1 -> x0, waiting for transfers between devices: 161 us -> none  [body(): lax.psum_scatter(jnp.transpose(term_rows, (2, 0, 1, 3)), 'space', scatter...]
    dot_general x162 -> x0, matrix products: 99.3 us -> none  [the longest x54 36.3 us: conv_transposed(): jnp.einsum('io,soxn->sixn', kernel[tap_index], shifted, preferred_element...]
    pallas_call x0 -> x1, Pallas kernels: none -> 59.2 us  [body(): pl.pallas_call(functools.partial(kernel, nd, ns, scale_a, scale_b), out_s...]
    all_gather x1 -> x0, blocking collectives: 38.8 us -> none  [body(): gathered = lax.all_gather(pooled, 'space', axis=2, tiled=True)]
    all_to_all x1 -> x0, starting transfers between devices: 12.8 us -> none  [body(): lax.all_to_all(upstream, 'space', split_axis=1, concat_axis=2, tiled=True)]
    ppermute x4 -> x0, starting transfers between devices: 8.69 us -> none  [the longest x2 6.11 us: with_halo(): before = lax.ppermute(last, axis, up)]
  transfers between devices with their start and end apart: 8 -> 0, of which waited for: 4 -> 0; matrix products, arithmetic and copies ran while one was open for 8% -> 0% of each run, Pallas kernels for 0% -> 0%
where the time goes in v1:
time: 66 us; the launch traced here: 65.8 us
  Pallas kernels  59.2 us (90%)
  local copies, waits for them, and re-layouts  4.06 us (6%)
  other arithmetic  1.86 us (3%)
  between operations  0.67 us (1%)
    pallas_call x1, Pallas kernels, body(): pl.pallas_call(functools.partial(kernel, nd, ns, scale_a, scale_b), out_s...  59.2 us
    unnamed x6, local copies, waits for them, and re-layouts  2.18 us
    convert_element_type x3, local copies, waits for them, and re-layouts, body(): jnp.transpose(gb, (2, 0, 3, 1)).reshape(27, 128, 256 // ns).astype(F32)  1.88 us

profile of v1, /device:TPU:1, one launch (start us, length us, event | category | flops | bytes accessed | tf_op | source)
XLA Modules:
  0.0 65.8 jit_solution(2264152158395167076)
XLA Ops:
  0.6 1.5 %copy.16 = bf16[1,64,2,256]{3,1,2,0:T(8,128)(2,1)} copy(bf16[1,64,2,256]{3,2,1,0:T(2,128)(2,1)} %param.4) | data formatting | bytes 131072 | tf_op args[0]
  2.1 59.2 %shard_map.67 = (bf16[2,64,256]{2,1,0:T(8,128)(2,1)}, bf16[8,32,1,8,128]{4,3,2,1,0:T(8,128)(2,1)}, bf16[8,8,512]{2,1,0:T(8,128)(2,1)}) custom-call(bf16[2,64,256]{2,1,0:T(8,128)(2,1)} %bitcast.28, bf16[9,192,128]{2,1,0:T(8,128)(2,1)} %bitcast.26, bf16[3,1152,256]{2,1,0:T(8,128)(2,1)} %bitcast.25, bf16[64,256]{1,0:T(8,128)(2,1)} %bitcast.30), custom_call_target="tpu_custom_call" | custom-call | tf_op jit(solution)/shard_map/pallas_call | solution.py:317
  61.3 0.9 %slice_convert_fusion = f32[8,8,432]{2,1,0:T(8,128)S(1)} fusion(bf16[8,8,512]{2,1,0:T(8,128)(2,1)} %get-tuple-element.8), kind=kLoop, calls=%fused_computation.3 | loop fusion | flops 27648 | bytes 165888 | tf_op jit(solution)/shard_map/convert_element_type | solution.py:362
  62.2 0.0 copy-start
  62.2 0.5 reshape.29
  62.6 0.0 copy-start.1
  62.6 0.5 copy.12
  63.2 0.9 %reshape.28 = f32[27,128,8]{1,2,0:T(8,128)} reshape(f32[27,8,16,8]{2,1,3,0:T(8,128)S(1)} %copy.12) | data formatting | bytes 221184 | tf_op jit(solution)/shard_map/convert_element_type | solution.py:362
  64.1 0.0 copy-done
  64.1 1.0 %copy_bitcast_fusion = f32[27,64,128]{2,1,0:T(8,128)} fusion(bf16[8,32,8,128]{3,2,1,0:T(8,128)(2,1)S(1)} %bitcast.27), kind=kLoop, calls=%fused_computation | loop fusion | flops 221184 | bytes 1327104 | tf_op jit(solution)/shard_map/convert_element_type | solution.py:360
  65.1 0.0 copy-done.1
  65.1 0.7 %copy.13 = bf16[1,64,2,256]{3,2,1,0:T(2,128)(2,1)} copy(bf16[1,64,2,256]{3,1,2,0:T(8,128)(2,1)S(1)} %bitcast.29) | data formatting | bytes 131072
Async XLA Ops:
  62.2 1.9 %copy-start = (bf16[8,32,1,8,128]{4,3,2,1,0:T(8,128)(2,1)S(1)}, bf16[8,32,1,8,128]{4,3,2,1,0:T(8,128)(2,1)}, u32[]{:S(2)}) copy-start(bf16[8,32,1,8,128]{4,3,2,1,0:T(8,128)(2,1)} %get-tuple-element.7) | copy-start | bytes 1572868
  62.6 2.5 %copy-start.1 = (bf16[2,64,256]{2,1,0:T(8,128)(2,1)S(1)}, bf16[2,64,256]{2,1,0:T(8,128)(2,1)}, u32[]{:S(2)}) copy-start(bf16[2,64,256]{2,1,0:T(8,128)(2,1)} %get-tuple-element.6) | copy-start | bytes 196612

commit v2 on v1

v2 whole, which is shorter than its diff:
```python
import functools
import math

import jax
import jax.numpy as jnp
from jax import lax
from jax.experimental import pallas as pl
from jax.experimental.pallas import tpu as pltpu
from jax.sharding import PartitionSpec as P

GY = 16
GZ = 16
CELLS = GY * GZ
HY = GY // 2
HZ = GZ // 2
POOL = HY * HZ
MESH = pl.DeviceIdType.MESH
F32 = jnp.float32
BF16 = jnp.bfloat16

NC = 2
NX = 4

(
    X_R, X_L, U_R, U_L, P_R, P_L, P_RR, P_LL, A_R, A_L, BP_Y, BG_Y, BP_C, BG_C,
    A_C, A_YX, A_Z, A_OUT, A_OUT_C, B_X, B_Z, B_OUT, N_SEM,
) = range(23)


def sigmoid(value):
    return 1.0 / (1.0 + jnp.exp(-value))


def slope(value, sigma):
    return sigma * (1.0 + value * (1.0 - sigma))


def shift_column(value, step, span):
    if step == 0:
        return value
    rows = value.shape[0]
    column = lax.broadcasted_iota(jnp.int32, value.shape, 0) % span + step
    moved = pltpu.roll(value, (-step) % rows, 0)
    return jnp.where((column >= 0) & (column < span), moved, 0.0)


def shift_block(value, step):
    if step == 0:
        return value
    zeros = jnp.zeros((abs(step), value.shape[1]), value.dtype)
    if step > 0:
        return jnp.concatenate([value[step:], zeros], axis=0)
    return jnp.concatenate([zeros, value[:step]], axis=0)


def kernel(
    nd, ns, scale_a, scale_b,
    x_hbm, wa_hbm, wb_hbm, up_hbm,
    gi_ref, ga_ref, gb_ref,
    x_raw, wa_ref, wb_ref, up_ref, xown, xh, uph, xz, slope_a, act_a, pown, ph, gbown,
    gaown, gah, gz, kr, spread,
    psend, py, pc, gy, gc, pcol, ac_send, ac_recv, ayx_send, ayx_recv, az, aout,
    bx_send, bx_recv, bz_send, bz_recv, bag, load, send, recv,
):
    ny, nz = nd // NC, ns // NX
    s = lax.axis_index("space")
    d = lax.axis_index("dp")
    y, c = d // NC, d % NC
    z, x = s // NX, s % NX
    right = lax.rem(s + 1, ns)
    left = lax.rem(s + ns - 1, ns)
    right2 = lax.rem(s + 2, ns)
    left2 = lax.rem(s + ns - 2, ns)
    has_left = s > 0
    has_right = s < ns - 1
    has_left2 = s > 1
    has_right2 = s < ns - 2
    core = {"dp": y * NC + 1 - c}

    loads = [
        pltpu.make_async_copy(src, dst, load.at[i])
        for i, (src, dst) in enumerate(
            ((x_hbm, x_raw), (up_hbm, up_ref), (wa_hbm, wa_ref), (wb_hbm, wb_ref))
        )
    ]
    for copy in loads:
        copy.start()

    def yx_device(k):
        k_y, k_x = k // NX, k % NX
        return {"dp": lax.rem(y + k_y, ny) * NC + c, "space": z * NX + lax.rem(x + k_x, NX)}

    def z_device(k):
        return {"space": lax.rem(z + k, nz) * NX + x}

    barrier = pltpu.get_barrier_semaphore()

    def greet(device):
        pl.semaphore_signal(barrier, inc=1, device_id=device, device_id_type=MESH)

    for near in (right, left, right2, left2):
        greet({"space": near})

    def greet_yx(k, carry):
        greet(yx_device(k))
        return carry

    def greet_z(k, carry):
        greet(z_device(k))
        return carry

    def greet_dp(k, carry):
        greet({"dp": lax.rem(d + k, nd)})
        return carry

    lax.fori_loop(1, nz, greet_z, 0)
    lax.fori_loop(1, ny * NX, greet_yx, 0)
    lax.fori_loop(1, nd, greet_dp, 0)

    loads[0].wait()
    both = x_raw[...].astype(F32)
    planes = [both[:, 0, :], both[:, 1, :]]
    for q in range(2):
        xown[q] = planes[q].astype(BF16)
    for q in range(4):
        xz[q, 0:GZ, :] = jnp.zeros((GZ, 192), BF16)
        xz[q, GZ + CELLS : 2 * GZ + CELLS, :] = jnp.zeros((GZ, 192), BF16)
        gz[q, 0:GZ, :] = jnp.zeros((GZ, 384), BF16)
        gz[q, GZ + CELLS : 2 * GZ + CELLS, :] = jnp.zeros((GZ, 384), BF16)

    def put_xz(q, plane):
        rows = plane.T
        wide = jnp.concatenate([shift_column(rows, -1, GZ), rows, shift_column(rows, 1, GZ)], axis=1)
        xz[q, GZ : GZ + CELLS, :] = wide.astype(BF16)

    put_xz(1, planes[0])
    put_xz(2, planes[1])
    loads[1].wait()
    loads[2].wait()
    for t in range(9):
        for j in range(3):
            kr[t, :, j * 128 : (j + 1) * 128] = wa_ref[t, j * 64 : (j + 1) * 64, :]

    def conv_a_terms(q, exs):
        total = None
        for ex in exs:
            for ey in range(3):
                part = jnp.dot(
                    xz[q + ex, ey * GZ : ey * GZ + CELLS, :], wa_ref[ex * 3 + ey],
                    preferred_element_type=F32,
                )
                total = part if total is None else total + part
        return total

    pl.semaphore_wait(barrier, 4 + (nz - 1) + (ny * NX - 1) + (nd - 1))

    def remote(src, dst, slot, device):
        return pltpu.make_async_remote_copy(
            src_ref=src, dst_ref=dst, send_sem=send.at[slot], recv_sem=recv.at[slot],
            device_id=device, device_id_type=MESH,
        )

    started = []

    def start(src, dst, slot, device):
        copy = remote(src, dst, slot, device)
        copy.start()
        started.append(copy)
        return copy

    def wait_part(sems, slot, part):
        pltpu.make_async_copy(part, part, sems.at[slot]).wait()

    x_halo = [start(xown.at[1], xh.at[0], X_R, {"space": right}), start(xown.at[0], xh.at[1], X_L, {"space": left})]
    u_halo = [start(up_ref, uph.at[0], U_R, {"space": right}), start(up_ref, uph.at[1], U_L, {"space": left})]

    act_a[0:CELLS, :] = conv_a_terms(0, (1, 2))
    act_a[CELLS : 2 * CELLS, :] = conv_a_terms(1, (0, 1))
    x_halo[0].wait_recv()
    put_xz(0, jnp.where(has_left, xh[0].astype(F32), 0.0))
    x_halo[1].wait_recv()
    put_xz(3, jnp.where(has_right, xh[1].astype(F32), 0.0))
    for q in range(2):
        area = slice(q * CELLS, (q + 1) * CELLS)
        pre = act_a[area, :] + conv_a_terms(q, (0,) if q == 0 else (2,))
        sigma = sigmoid(pre)
        act_a[area, :] = pre * sigma
        slope_a[area, :] = slope(pre, sigma) * 0.125

    pairs = act_a[pl.ds(0, CELLS, stride=2), :] + act_a[pl.ds(1, CELLS, stride=2), :]
    pairs = pairs.reshape(2, HY, 2, HZ, 128)
    pooled = (pairs[0, :, 0] + pairs[0, :, 1] + pairs[1, :, 0] + pairs[1, :, 1]).reshape(POOL, 128) * 0.125
    pown[...] = pooled.astype(BF16)
    p_halo = [
        start(pown, ph.at[0], P_RR, {"space": right2}),
        start(pown, ph.at[3], P_LL, {"space": left2}),
        start(pown, ph.at[1], P_R, {"space": right}),
        start(pown, ph.at[2], P_L, {"space": left}),
    ]

    def taps_of(plane):
        moved = [shift_column(plane, step, HZ) for step in (-1, 0, 1)]
        taps = []
        for ey in range(3):
            for ez in range(3):
                taps.append(shift_block(moved[ez], (ey - 1) * HZ).astype(BF16))
        return jnp.concatenate(taps, axis=1)

    own_p = pown[...].astype(F32)
    own_taps = taps_of(own_p)
    loads[3].wait()
    p_halo[2].wait_recv()
    p_halo[3].wait_recv()
    left_p = jnp.where(has_left, ph[1].astype(F32), 0.0)
    right_p = jnp.where(has_right, ph[2].astype(F32), 0.0)

    chans = 128 // nd
    for e, plane in enumerate((left_p, own_p, right_p)):
        psend[:, :, e] = plane.T.reshape(NC, ny, chans, POOL).astype(BF16)
    for cc in range(NC):
        py[cc, y] = psend[cc, y]

    def p_step(k, carry):
        other = lax.rem(y + k, ny)
        for cc in range(NC):
            remote(psend.at[cc, other], py.at[cc, y], BP_Y, {"dp": other * NC + c}).start()
        return carry

    lax.fori_loop(1, ny, p_step, 0)
    left_taps = taps_of(left_p)
    right_taps = taps_of(right_p)
    p_halo[0].wait_recv()
    p_halo[1].wait_recv()
    left2_taps = taps_of(jnp.where(has_left2, ph[0].astype(F32), 0.0))
    right2_taps = taps_of(jnp.where(has_right2, ph[3].astype(F32), 0.0))
    order = (left2_taps, left_taps, own_taps, right_taps, right2_taps)
    pre_b = None
    for ex in range(3):
        part = jnp.dot(jnp.concatenate(order[ex : ex + 3], axis=0), wb_ref[ex], preferred_element_type=F32)
        pre_b = part if pre_b is None else pre_b + part
    slope_b = slope(pre_b, sigmoid(pre_b))
    own_g = (up_ref[...].astype(F32) * slope_b[POOL : 2 * POOL]).astype(BF16)
    gbown[...] = own_g
    gy[y] = own_g

    def g_step(k, carry):
        remote(gbown, gy.at[y], BG_Y, {"dp": lax.rem(y + k, ny) * NC + c}).start()
        return carry

    lax.fori_loop(1, ny, g_step, 0)
    u_halo[0].wait_recv()
    u_halo[1].wait_recv()
    left_g = jnp.where(has_left, uph[0].astype(F32) * slope_b[0:POOL], 0.0).astype(BF16)
    right_g = jnp.where(has_right, uph[1].astype(F32) * slope_b[2 * POOL :], 0.0).astype(BF16)

    grad_pool = None
    for ex, plane in ((0, right_g), (1, own_g), (2, left_g)):
        wide = plane.astype(F32)
        moved = [shift_column(wide, -step, HZ) for step in (-1, 0, 1)]
        for ey in range(3):
            for ez in range(3):
                tap = ey * 3 + ez
                shifted = shift_block(moved[ez], -(ey - 1) * HZ).astype(BF16)
                part = lax.dot_general(
                    shifted, wb_ref[ex, tap * 128 : (tap + 1) * 128, :],
                    (((1,), (1,)), ((), ())), preferred_element_type=F32,
                )
                grad_pool = part if grad_pool is None else grad_pool + part

    tall = jnp.broadcast_to(grad_pool.reshape(HY, 1, HZ, 128), (HY, 2, HZ, 128)).reshape(GY * HZ, 128)
    spread[pl.ds(0, GY * HZ, stride=2), :] = tall
    spread[pl.ds(1, GY * HZ, stride=2), :] = tall
    for q in range(2):
        gaown[q] = (spread[...] * slope_a[q * CELLS : (q + 1) * CELLS, :]).astype(BF16)
    a_halo = [start(gaown.at[1], gah.at[0], A_R, {"space": right}), start(gaown.at[0], gah.at[1], A_L, {"space": left})]

    rows_a = 64 // nd
    taps_x = ac_send.shape[3]
    grads = [gaown[0], gaown[1]]
    for tap in range(27, taps_x * NX):
        ac_send[:, :, tap // taps_x, tap % taps_x] = jnp.zeros((NC, ny, rows_a, 128), BF16)
    for ex in range(3):
        for ey in range(3):
            term = None
            for q in range(2):
                part = lax.dot_general(
                    xz[q + ex, ey * GZ : ey * GZ + CELLS, :], grads[q],
                    (((0,), (0,)), ((), ())), preferred_element_type=F32,
                )
                term = part if term is None else term + part
            for ez in range(3):
                tap = ex * 9 + ey * 3 + ez
                ac_send[:, :, tap // taps_x, tap % taps_x] = (
                    term[ez * 64 : (ez + 1) * 64, :].reshape(NC, ny, rows_a, 128).astype(BF16)
                )
    a_core = start(ac_send.at[1 - c], ac_recv, A_C, core)

    def put_gz(q, plane):
        wide = jnp.concatenate([shift_column(plane, 1, GZ), plane, shift_column(plane, -1, GZ)], axis=1)
        gz[q, GZ : GZ + CELLS, :] = wide.astype(BF16)

    put_gz(1, gaown[0].astype(F32))
    put_gz(2, gaown[1].astype(F32))

    a_core.wait_recv()
    ayx_send[...] = (ac_send[c].astype(F32) + ac_recv[...].astype(F32)).astype(BF16)
    me_yx = y * NX + x
    ayx_recv[me_yx] = ayx_send[y, x]

    def yx_step(k, carry):
        k_y, k_x = k // NX, k % NX
        remote(
            ayx_send.at[lax.rem(y + k_y, ny), lax.rem(x + k_x, NX)], ayx_recv.at[me_yx], A_YX, yx_device(k)
        ).start()
        return carry

    lax.fori_loop(1, ny * NX, yx_step, 0)

    wait_part(recv, BP_Y, py.at[:, pl.ds(0, ny - 1)])
    bp_core = start(py.at[1 - c], pc, BP_C, core)
    wait_part(recv, BG_Y, gy.at[pl.ds(0, ny - 1)])
    bg_core = start(gy, gc, BG_C, core)

    def conv_at(q, exs, total):
        for ex in exs:
            for ey in range(3):
                part = lax.dot_general(
                    kr[ex * 3 + ey], gz[q + 2 - ex, (2 - ey) * GZ : (2 - ey) * GZ + CELLS, :],
                    (((1,), (1,)), ((), ())), preferred_element_type=F32,
                )
                total = part if total is None else total + part
        return total

    a_halo[0].wait_recv()
    put_gz(0, jnp.where(has_left, gah[0].astype(F32), 0.0))
    a_halo[1].wait_recv()
    put_gz(3, jnp.where(has_right, gah[1].astype(F32), 0.0))

    bp_core.wait_recv()
    bg_core.wait_recv()
    half = ny * POOL
    lane = lax.broadcasted_iota(jnp.int32, (chans, NC * half), 1)
    row = lane // HZ % HY
    column = lane % HZ
    for ex in range(3):
        flat = jnp.concatenate(
            [py[c, n, ex].astype(F32) for n in range(ny)] + [pc[n, ex].astype(F32) for n in range(ny)], axis=1
        )
        for ey in range(3):
            for ez in range(3):
                step = (ey - 1) * HZ + ez - 1
                inside = (row + ey - 1 >= 0) & (row + ey - 1 < HY) & (column + ez - 1 >= 0) & (column + ez - 1 < HZ)
                moved = flat if step == 0 else pltpu.roll(flat, (-step) % (NC * half), 1)
                tap = ex * 9 + ey * 3 + ez
                pcol[tap * chans : (tap + 1) * chans, :] = jnp.where(inside, moved, 0.0).astype(BF16)
    used = 27 * chans
    padded = pcol.shape[0]
    if padded > used:
        pcol[used:padded, :] = jnp.zeros((padded - used, NC * half), BF16)
    part_b = jnp.dot(pcol[:, 0:half], gy[...].reshape(half, 256), preferred_element_type=F32)
    part_b = part_b + jnp.dot(pcol[:, half:], gc[...].reshape(half, 256), preferred_element_type=F32)
    part_b = part_b.T.reshape(nz, NX, 256 // ns, padded).astype(BF16)
    for xx in range(NX):
        bx_send[xx] = part_b[:, xx]
    bx_recv[x] = bx_send[x]

    def bx_step(k, carry):
        other = lax.rem(x + k, NX)
        remote(bx_send.at[other], bx_recv.at[x], B_X, {"space": z * NX + other}).start()
        return carry

    lax.fori_loop(1, NX, bx_step, 0)

    for q in range(2):
        gi_ref[:, q, :] = conv_at(q, (0, 1, 2), None).astype(BF16)

    wait_part(recv, A_YX, ayx_recv.at[pl.ds(0, ny * NX - 1)])
    total = ayx_recv[0].astype(F32)
    for n in range(1, ny * NX):
        total = total + ayx_recv[n].astype(F32)
    az[z] = total.astype(BF16)

    def z_step(k, carry):
        remote(az.at[z], az.at[z], A_Z, z_device(k)).start()
        return carry

    lax.fori_loop(1, nz, z_step, 0)

    wait_part(recv, B_X, bx_recv.at[pl.ds(0, NX - 1)])
    total_b = bx_recv[0].astype(F32)
    for n in range(1, NX):
        total_b = total_b + bx_recv[n].astype(F32)
    bz_send[...] = total_b.astype(BF16)
    bz_recv[z] = bz_send[z]

    def bz_step(k, carry):
        other = lax.rem(z + k, nz)
        remote(bz_send.at[other], bz_recv.at[z], B_Z, {"space": other * NX + x}).start()
        return carry

    lax.fori_loop(1, nz, bz_step, 0)

    wait_part(recv, A_Z, az.at[pl.ds(0, nz - 1)])
    total = az[0].astype(F32)
    for n in range(1, nz):
        total = total + az[n].astype(F32)
    aout[c, me_yx] = (total * scale_a).astype(BF16)

    def out_step(k, carry):
        remote(aout.at[c, me_yx], aout.at[c, me_yx], A_OUT, yx_device(k)).start()
        return carry

    lax.fori_loop(1, ny * NX, out_step, 0)

    wait_part(recv, B_Z, bz_recv.at[pl.ds(0, nz - 1)])
    total_b = bz_recv[0].astype(F32)
    for n in range(1, nz):
        total_b = total_b + bz_recv[n].astype(F32)
    slice_b = c * ny + y
    bag[slice_b] = (total_b * scale_b).astype(BF16)

    def bag_step(k, carry):
        remote(bag.at[slice_b], bag.at[slice_b], B_OUT, {"dp": lax.rem(d + k, nd)}).start()
        return carry

    lax.fori_loop(1, nd, bag_step, 0)

    wait_part(recv, A_OUT, aout.at[0, pl.ds(0, ny * NX - 1)])
    a_out_core = start(aout.at[c], aout.at[c], A_OUT_C, core)

    wait_part(recv, B_OUT, bag.at[pl.ds(0, nd - 1)])
    for tap in range(27):
        gb_ref[tap] = jnp.concatenate(
            [bag[e, :, tap * chans : (tap + 1) * chans].astype(F32) for e in range(nd)], axis=1
        )
    a_out_core.wait_recv()
    ga_ref[...] = aout[...]

    for copy in started:
        copy.wait_send()
    wait_part(send, BP_Y, py.at[:, pl.ds(0, ny - 1)])
    wait_part(send, BG_Y, gy.at[pl.ds(0, ny - 1)])
    wait_part(send, A_YX, ayx_recv.at[pl.ds(0, ny * NX - 1)])
    wait_part(send, A_Z, az.at[pl.ds(0, nz - 1)])
    wait_part(send, A_OUT, ayx_recv.at[pl.ds(0, ny * NX - 1)])
    wait_part(send, B_X, bx_recv.at[pl.ds(0, NX - 1)])
    wait_part(send, B_Z, bz_recv.at[pl.ds(0, nz - 1)])
    wait_part(send, B_OUT, bag.at[pl.ds(0, nd - 1)])


def body(nd, ns, scale_a, scale_b, features, kernel_a, kernel_b, upstream):
    wa = kernel_a.reshape(9, 192, 128)
    wb = kernel_b.reshape(3, 9 * 128, 256)
    up = upstream[0, :, 0, :].T
    ny, nz = nd // NC, ns // NX
    rows_a = 64 // nd
    chans = 128 // nd
    filters = 256 // ns
    taps_x = -(-27 // NX)
    padded = -(-27 * chans // 128) * 128
    vmem = pl.BlockSpec(memory_space=pltpu.VMEM)
    hbm = pl.BlockSpec(memory_space=pl.ANY)
    block_a = (taps_x, rows_a, 128)
    gi, ga, gb = pl.pallas_call(
        functools.partial(kernel, nd, ns, scale_a, scale_b),
        out_shape=(
            jax.ShapeDtypeStruct((64, 2, CELLS), BF16),
            jax.ShapeDtypeStruct((NC, ny * NX) + block_a, BF16),
            jax.ShapeDtypeStruct((27, filters, 128), F32),
        ),
        in_specs=[hbm] * 4,
        out_specs=(vmem, vmem, vmem),
        scratch_shapes=[
            pltpu.VMEM((64, 2, CELLS), BF16),
            pltpu.VMEM((9, 192, 128), BF16),
            pltpu.VMEM((3, 9 * 128, 256), BF16),
            pltpu.VMEM((POOL, 256), BF16),
            pltpu.VMEM((2, 64, CELLS), BF16),
            pltpu.VMEM((2, 64, CELLS), BF16),
            pltpu.VMEM((2, POOL, 256), BF16),
            pltpu.VMEM((4, CELLS + 2 * GZ, 192), BF16),
            pltpu.VMEM((2 * CELLS, 128), F32),
            pltpu.VMEM((2 * CELLS, 128), F32),
            pltpu.VMEM((POOL, 128), BF16),
            pltpu.VMEM((4, POOL, 128), BF16),
            pltpu.VMEM((POOL, 256), BF16),
            pltpu.VMEM((2, CELLS, 128), BF16),
            pltpu.VMEM((2, CELLS, 128), BF16),
            pltpu.VMEM((4, CELLS + 2 * GZ, 384), BF16),
            pltpu.VMEM((9, 64, 384), BF16),
            pltpu.VMEM((CELLS, 128), F32),
            pltpu.VMEM((NC, ny, 3, chans, POOL), BF16),
            pltpu.VMEM((NC, ny, 3, chans, POOL), BF16),
            pltpu.VMEM((ny, 3, chans, POOL), BF16),
            pltpu.VMEM((ny, POOL, 256), BF16),
            pltpu.VMEM((ny, POOL, 256), BF16),
            pltpu.VMEM((padded, nd * POOL), BF16),
            pltpu.VMEM((NC, ny, NX) + block_a, BF16),
            pltpu.VMEM((ny, NX) + block_a, BF16),
            pltpu.VMEM((ny, NX) + block_a, BF16),
            pltpu.VMEM((ny * NX,) + block_a, BF16),
            pltpu.VMEM((nz,) + block_a, BF16),
            pltpu.VMEM((NC, ny * NX) + block_a, BF16),
            pltpu.VMEM((NX, nz, filters, padded), BF16),
            pltpu.VMEM((NX, nz, filters, padded), BF16),
            pltpu.VMEM((nz, filters, padded), BF16),
            pltpu.VMEM((nz, filters, padded), BF16),
            pltpu.VMEM((nd, filters, padded), BF16),
            pltpu.SemaphoreType.DMA((4,)),
            pltpu.SemaphoreType.DMA((N_SEM,)),
            pltpu.SemaphoreType.DMA((N_SEM,)),
        ],
        compiler_params=pltpu.CompilerParams(collective_id=0, has_side_effects=True),
    )(features[0], wa, wb, up)
    ga = ga.reshape(NC, ny, NX * taps_x, rows_a, 128)[:, :, :27]
    grad_a = jnp.transpose(ga, (2, 0, 1, 3, 4)).reshape(27, 64, 128).astype(F32)
    return gi[None], grad_a, jnp.transpose(gb, (0, 2, 1))


def solution(mesh):
    nd, ns = mesh.shape["dp"], mesh.shape["space"]
    cells_all = nd * 2 * ns * CELLS
    run = functools.partial(body, nd, ns, 1.0 / math.sqrt(cells_all), 1.0 / math.sqrt(cells_all / 8))
    return jax.shard_map(
        run,
        mesh=mesh,
        in_specs=(P("dp", None, "space", None), P(), P(), P("dp", None, "space", None)),
        out_specs=(P("dp", None, "space", None), P(), P(None, None, "space")),
        check_vma=False,
    )
```

time: 66 us -> 50.3 us (0.76)
  Pallas kernels: 59.2 us -> 46.1 us
  local copies, waits for them, and re-layouts: 4.06 us -> 2.31 us
  other arithmetic: 1.86 us -> 1.11 us
    pallas_call x1, Pallas kernels: 59.2 us -> 46.1 us  [body(): pl.pallas_call(functools.partial(kernel, nd, ns, scale_a, scale_b), out_s...]
    unnamed x6, local copies, waits for them, and re-layouts: 2.18 us -> 1.28 us
    convert_element_type x3 -> x1, local copies, waits for them, and re-layouts: 1.88 us -> 1.03 us  [body(): grad_a = jnp.transpose(ga, (2, 0, 1, 3, 4)).reshape(27, 64, 128).astype(F32)]
    convert_element_type x2 -> x1, other arithmetic: 1.86 us -> 1.11 us  [body(): grad_a = jnp.transpose(ga, (2, 0, 1, 3, 4)).reshape(27, 64, 128).astype(F32)]
where the time goes in v2:
time: 50.3 us; the launch traced here: 50.2 us
  Pallas kernels  46.1 us (92%)
  local copies, waits for them, and re-layouts  2.31 us (5%)
  other arithmetic  1.11 us (2%)
  between operations  0.66 us (1%)
    pallas_call x1, Pallas kernels, body(): pl.pallas_call(functools.partial(kernel, nd, ns, scale_a, scale_b), out_s...  46.1 us
    unnamed x6, local copies, waits for them, and re-layouts  1.28 us
    convert_element_type x1, other arithmetic, body(): grad_a = jnp.transpose(ga, (2, 0, 1, 3, 4)).reshape(27, 64, 128).astype(F32)  1.11 us
    convert_element_type x1, local copies, waits for them, and re-layouts, body(): grad_a = jnp.transpose(ga, (2, 0, 1, 3, 4)).reshape(27, 64, 128).astype(F32)  1.03 us

profile of v2, /device:TPU:1, one launch (start us, length us, event | category | flops | bytes accessed | tf_op | source)
XLA Modules:
  0.0 50.2 jit_solution(1935882844685623186)
XLA Ops:
  0.6 46.1 %shard_map.67 = (bf16[64,2,256]{2,1,0:T(2,128)(2,1)}, bf16[2,16,7,8,128]{4,3,2,1,0:T(8,128)(2,1)}, f32[27,8,128]{2,1,0:T(8,128)}) custom-call(bf16[64,2,256]{2,1,0:T(2,128)(2,1)} %bitcast.17, bf16[9,192,128]{2,1,0:T(8,128)(2,1)} %bitcast.14, bf16[3,1152,256]{2,1,0:T(8,128)(2,1)} %bitcast.12, bf16[64,256]{1,0:T(8,128)(2,1)} %bitcast.19), custom_call_target="tpu_custom_call" | custom-call | tf_op jit(solution)/shard_map/pallas_call | solution.py:464
  46.8 0.0 copy-start.1
  46.8 0.0 copy-start
  46.8 1.1 %convert_bitcast_fusion = f32[27,2,4,8,128]{4,3,0,2,1:T(8,128)S(1)} fusion(bf16[2,4,28,8,128]{4,3,2,1,0:T(8,128)(2,1)} %bitcast.15), kind=kLoop, calls=%fused_computation | loop fusion | flops 221184 | bytes 1327104 | tf_op jit(solution)/shard_map/convert_element_type | solution.py:516
  47.9 1.0 %copy.7 = f32[27,2,4,8,128]{4,3,2,1,0:T(8,128)} copy(f32[27,2,4,8,128]{4,3,0,2,1:T(8,128)S(1)} %convert_bitcast_fusion) | data formatting | bytes 1769472 | tf_op jit(solution)/shard_map/convert_element_type | solution.py:516
  48.9 0.0 copy-done.1
  48.9 0.6 %copy.10 = bf16[1,64,2,256]{3,2,1,0:T(2,128)(2,1)} copy(bf16[1,64,2,256]{3,2,1,0:T(2,128)(2,1)S(1)} %bitcast.18) | data formatting | bytes 131072
  49.6 0.0 copy-done
  49.6 0.6 %copy.11 = f32[27,128,8]{1,2,0:T(8,128)} copy(f32[27,128,8]{1,2,0:T(8,128)S(1)} %bitcast.16) | data formatting | bytes 221184
Async XLA Ops:
  46.8 2.2 %copy-start.1 = (bf16[64,2,256]{2,1,0:T(2,128)(2,1)S(1)}, bf16[64,2,256]{2,1,0:T(2,128)(2,1)}, u32[]{:S(2)}) copy-start(bf16[64,2,256]{2,1,0:T(2,128)(2,1)} %get-tuple-element.6) | copy-start | bytes 196612
  46.8 2.8 %copy-start = (f32[27,8,128]{2,1,0:T(8,128)S(1)}, f32[27,8,128]{2,1,0:T(8,128)}, u32[]{:S(2)}) copy-start(f32[27,8,128]{2,1,0:T(8,128)} %get-tuple-element.8) | copy-start | bytes 331780

commit v3 on v2

--- a/solution.py
+++ b/solution.py
@@ -57,7 +57,7 @@
     nd, ns, scale_a, scale_b,
     x_hbm, wa_hbm, wb_hbm, up_hbm,
     gi_ref, ga_ref, gb_ref,
-    x_raw, wa_ref, wb_ref, up_ref, xown, xh, uph, xz, slope_a, act_a, pown, ph, gbown,
+    x_raw, wa_ref, wb_ref, up_ref, xown, xh, uph, xz, xt, slope_a, act_a, pown, ph, gbown,
     gaown, gah, gz, kr, spread,
     psend, py, pc, gy, gc, pcol, ac_send, ac_recv, ayx_send, ayx_recv, az, aout,
     bx_send, bx_recv, bz_send, bz_recv, bag, load, send, recv,
@@ -198,6 +198,11 @@
         start(pown, ph.at[2], P_L, {"space": left}),
     ]
 
+    for q in range(4):
+        for ey in range(3):
+            rows = xz[q, ey * GZ : ey * GZ + CELLS, :].astype(F32)
+            xt[q, ey * 192 : (ey + 1) * 192, :] = rows.T.astype(BF16)
+
     def taps_of(plane):
         moved = [shift_column(plane, step, HZ) for step in (-1, 0, 1)]
         taps = []
@@ -253,19 +258,21 @@
     left_g = jnp.where(has_left, uph[0].astype(F32) * slope_b[0:POOL], 0.0).astype(BF16)
     right_g = jnp.where(has_right, uph[1].astype(F32) * slope_b[2 * POOL :], 0.0).astype(BF16)
 
+    products = None
+    for ex, plane in ((0, right_g), (1, own_g), (2, left_g)):
+        part = lax.dot_general(
+            wb_ref[ex], plane, (((1,), (1,)), ((), ())), preferred_element_type=F32,
+        )
+        products = part if products is None else products + part
     grad_pool = None
-    for ex, plane in ((0, right_g), (1, own_g), (2, left_g)):
-        wide = plane.astype(F32)
-        moved = [shift_column(wide, -step, HZ) for step in (-1, 0, 1)]
+    for ez in range(3):
+        column = None
         for ey in range(3):
-            for ez in range(3):
-                tap = ey * 3 + ez
-                shifted = shift_block(moved[ez], -(ey - 1) * HZ).astype(BF16)
-                part = lax.dot_general(
-                    shifted, wb_ref[ex, tap * 128 : (tap + 1) * 128, :],
-                    (((1,), (1,)), ((), ())), preferred_element_type=F32,
-                )
-                grad_pool = part if grad_pool is None else grad_pool + part
+            tap = ey * 3 + ez
+            part = shift_block(products[tap * 128 : (tap + 1) * 128, :].T, -(ey - 1) * HZ)
+            column = part if column is None else column + part
+        column = shift_column(column, -(ez - 1), HZ)
+        grad_pool = column if grad_pool is None else grad_pool + column
 
     tall = jnp.broadcast_to(grad_pool.reshape(HY, 1, HZ, 128), (HY, 2, HZ, 128)).reshape(GY * HZ, 128)
     spread[pl.ds(0, GY * HZ, stride=2), :] = tall
@@ -280,19 +287,15 @@
     for tap in range(27, taps_x * NX):
         ac_send[:, :, tap // taps_x, tap % taps_x] = jnp.zeros((NC, ny, rows_a, 128), BF16)
     for ex in range(3):
-        for ey in range(3):
-            term = None
-            for q in range(2):
-                part = lax.dot_general(
-                    xz[q + ex, ey * GZ : ey * GZ + CELLS, :], grads[q],
-                    (((0,), (0,)), ((), ())), preferred_element_type=F32,
-                )
-                term = part if term is None else term + part
-            for ez in range(3):
-                tap = ex * 9 + ey * 3 + ez
-                ac_send[:, :, tap // taps_x, tap % taps_x] = (
-                    term[ez * 64 : (ez + 1) * 64, :].reshape(NC, ny, rows_a, 128).astype(BF16)
-                )
+        term = None
+        for q in range(2):
+            part = jnp.dot(xt[q + ex], grads[q], preferred_element_type=F32)
+            term = part if term is None else term + part
+        for t in range(9):
+            tap = ex * 9 + t
+            ac_send[:, :, tap // taps_x, tap % taps_x] = (
+                term[t * 64 : (t + 1) * 64, :].reshape(NC, ny, rows_a, 128).astype(BF16)
+            )
     a_core = start(ac_send.at[1 - c], ac_recv, A_C, core)
 
     def put_gz(q, plane):
@@ -479,6 +482,7 @@
             pltpu.VMEM((2, 64, CELLS), BF16),
             pltpu.VMEM((2, POOL, 256), BF16),
             pltpu.VMEM((4, CELLS + 2 * GZ, 192), BF16),
+            pltpu.VMEM((4, 576, CELLS), BF16),
             pltpu.VMEM((2 * CELLS, 128), F32),
             pltpu.VMEM((2 * CELLS, 128), F32),
             pltpu.VMEM((POOL, 128), BF16),

time: 50.3 us -> 50.4 us (level)
  no operation moved by 1% of the time
where the time goes in v3:
time: 50.4 us; the launch traced here: 50.3 us
  Pallas kernels  46.2 us (92%)
  local copies, waits for them, and re-layouts  2.31 us (5%)
  other arithmetic  1.11 us (2%)
  between operations  0.66 us (1%)
    pallas_call x1, Pallas kernels, body(): pl.pallas_call(functools.partial(kernel, nd, ns, scale_a, scale_b), out_s...  46.2 us
    unnamed x6, local copies, waits for them, and re-layouts  1.28 us
    convert_element_type x1, other arithmetic, body(): grad_a = jnp.transpose(ga, (2, 0, 1, 3, 4)).reshape(27, 64, 128).astype(F32)  1.11 us
    convert_element_type x1, local copies, waits for them, and re-layouts, body(): grad_a = jnp.transpose(ga, (2, 0, 1, 3, 4)).reshape(27, 64, 128).astype(F32)  1.03 us

profile of v3, /device:TPU:1, one launch (start us, length us, event | category | flops | bytes accessed | tf_op | source)
XLA Modules:
  0.0 50.3 jit_solution(8880211445353408074)
XLA Ops:
  0.6 46.2 %shard_map.67 = (bf16[64,2,256]{2,1,0:T(2,128)(2,1)}, bf16[2,16,7,8,128]{4,3,2,1,0:T(8,128)(2,1)}, f32[27,8,128]{2,1,0:T(8,128)}) custom-call(bf16[64,2,256]{2,1,0:T(2,128)(2,1)} %bitcast.17, bf16[9,192,128]{2,1,0:T(8,128)(2,1)} %bitcast.14, bf16[3,1152,256]{2,1,0:T(8,128)(2,1)} %bitcast.12, bf16[64,256]{1,0:T(8,128)(2,1)} %bitcast.19), custom_call_target="tpu_custom_call" | custom-call | tf_op jit(solution)/shard_map/pallas_call | solution.py:467
  46.8 0.0 copy-start.1
  46.8 0.0 copy-start
  46.9 1.1 %convert_bitcast_fusion = f32[27,2,4,8,128]{4,3,0,2,1:T(8,128)S(1)} fusion(bf16[2,4,28,8,128]{4,3,2,1,0:T(8,128)(2,1)} %bitcast.15), kind=kLoop, calls=%fused_computation | loop fusion | flops 221184 | bytes 1327104 | tf_op jit(solution)/shard_map/convert_element_type | solution.py:520
  48.0 1.0 %copy.7 = f32[27,2,4,8,128]{4,3,2,1,0:T(8,128)} copy(f32[27,2,4,8,128]{4,3,0,2,1:T(8,128)S(1)} %convert_bitcast_fusion) | data formatting | bytes 1769472 | tf_op jit(solution)/shard_map/convert_element_type | solution.py:520
  49.0 0.0 copy-done.1
  49.0 0.6 %copy.10 = bf16[1,64,2,256]{3,2,1,0:T(2,128)(2,1)} copy(bf16[1,64,2,256]{3,2,1,0:T(2,128)(2,1)S(1)} %bitcast.18) | data formatting | bytes 131072
  49.6 0.0 copy-done
  49.6 0.6 %copy.11 = f32[27,128,8]{1,2,0:T(8,128)} copy(f32[27,128,8]{1,2,0:T(8,128)S(1)} %bitcast.16) | data formatting | bytes 221184
Async XLA Ops:
  46.8 2.2 %copy-start.1 = (bf16[64,2,256]{2,1,0:T(2,128)(2,1)S(1)}, bf16[64,2,256]{2,1,0:T(2,128)(2,1)}, u32[]{:S(2)}) copy-start(bf16[64,2,256]{2,1,0:T(2,128)(2,1)} %get-tuple-element.6) | copy-start | bytes 196612
  46.8 2.8 %copy-start = (f32[27,8,128]{2,1,0:T(8,128)S(1)}, f32[27,8,128]{2,1,0:T(8,128)}, u32[]{:S(2)}) copy-start(f32[27,8,128]{2,1,0:T(8,128)} %get-tuple-element.8) | copy-start | bytes 331780

commit v4 on v3

--- a/solution.py
+++ b/solution.py
@@ -321,8 +321,6 @@
 
     wait_part(recv, BP_Y, py.at[:, pl.ds(0, ny - 1)])
     bp_core = start(py.at[1 - c], pc, BP_C, core)
-    wait_part(recv, BG_Y, gy.at[pl.ds(0, ny - 1)])
-    bg_core = start(gy, gc, BG_C, core)
 
     def conv_at(q, exs, total):
         for ex in exs:
@@ -334,18 +332,15 @@
                 total = part if total is None else total + part
         return total
 
-    a_halo[0].wait_recv()
-    put_gz(0, jnp.where(has_left, gah[0].astype(F32), 0.0))
-    a_halo[1].wait_recv()
-    put_gz(3, jnp.where(has_right, gah[1].astype(F32), 0.0))
-
     bp_core.wait_recv()
-    bg_core.wait_recv()
     half = ny * POOL
     lane = lax.broadcasted_iota(jnp.int32, (chans, NC * half), 1)
     row = lane // HZ % HY
     column = lane % HZ
     for ex in range(3):
+        if ex == 1:
+            wait_part(recv, BG_Y, gy.at[pl.ds(0, ny - 1)])
+            bg_core = start(gy, gc, BG_C, core)
         flat = jnp.concatenate(
             [py[c, n, ex].astype(F32) for n in range(ny)] + [pc[n, ex].astype(F32) for n in range(ny)], axis=1
         )
@@ -361,6 +356,7 @@
     if padded > used:
         pcol[used:padded, :] = jnp.zeros((padded - used, NC * half), BF16)
     part_b = jnp.dot(pcol[:, 0:half], gy[...].reshape(half, 256), preferred_element_type=F32)
+    bg_core.wait_recv()
     part_b = part_b + jnp.dot(pcol[:, half:], gc[...].reshape(half, 256), preferred_element_type=F32)
     part_b = part_b.T.reshape(nz, NX, 256 // ns, padded).astype(BF16)
     for xx in range(NX):
@@ -374,8 +370,10 @@
 
     lax.fori_loop(1, NX, bx_step, 0)
 
-    for q in range(2):
-        gi_ref[:, q, :] = conv_at(q, (0, 1, 2), None).astype(BF16)
+    a_halo[0].wait_recv()
+    put_gz(0, jnp.where(has_left, gah[0].astype(F32), 0.0))
+    a_halo[1].wait_recv()
+    put_gz(3, jnp.where(has_right, gah[1].astype(F32), 0.0))
 
     wait_part(recv, A_YX, ayx_recv.at[pl.ds(0, ny * NX - 1)])
     total = ayx_recv[0].astype(F32)
@@ -388,6 +386,8 @@
         return carry
 
     lax.fori_loop(1, nz, z_step, 0)
+
+    gi_ref[:, 0, :] = conv_at(0, (0, 1, 2), None).astype(BF16)
 
     wait_part(recv, B_X, bx_recv.at[pl.ds(0, NX - 1)])
     total_b = bx_recv[0].astype(F32)
@@ -402,6 +402,8 @@
         return carry
 
     lax.fori_loop(1, nz, bz_step, 0)
+
+    gi_ref[:, 1, :] = conv_at(1, (0, 1, 2), None).astype(BF16)
 
     wait_part(recv, A_Z, az.at[pl.ds(0, nz - 1)])
     total = az[0].astype(F32)

time: 50.4 us -> 50.3 us (level)
  no operation moved by 1% of the time
where the time goes in v4:
time: 50.3 us; the launch traced here: 50.1 us
  Pallas kernels  46.1 us (92%)
  local copies, waits for them, and re-layouts  2.31 us (5%)
  other arithmetic  1.11 us (2%)
  between operations  0.66 us (1%)
    pallas_call x1, Pallas kernels, body(): pl.pallas_call(functools.partial(kernel, nd, ns, scale_a, scale_b), out_s...  46.1 us
    unnamed x6, local copies, waits for them, and re-layouts  1.28 us
    convert_element_type x1, other arithmetic, body(): grad_a = jnp.transpose(ga, (2, 0, 1, 3, 4)).reshape(27, 64, 128).astype(F32)  1.11 us
    convert_element_type x1, local copies, waits for them, and re-layouts, body(): grad_a = jnp.transpose(ga, (2, 0, 1, 3, 4)).reshape(27, 64, 128).astype(F32)  1.03 us

profile of v4, /device:TPU:1, one launch (start us, length us, event | category | flops | bytes accessed | tf_op | source)
XLA Modules:
  0.0 50.1 jit_solution(15667079596687608864)
XLA Ops:
  0.6 46.1 %shard_map.67 = (bf16[64,2,256]{2,1,0:T(2,128)(2,1)}, bf16[2,16,7,8,128]{4,3,2,1,0:T(8,128)(2,1)}, f32[27,8,128]{2,1,0:T(8,128)}) custom-call(bf16[64,2,256]{2,1,0:T(2,128)(2,1)} %bitcast.17, bf16[9,192,128]{2,1,0:T(8,128)(2,1)} %bitcast.14, bf16[3,1152,256]{2,1,0:T(8,128)(2,1)} %bitcast.12, bf16[64,256]{1,0:T(8,128)(2,1)} %bitcast.19), custom_call_target="tpu_custom_call" | custom-call | tf_op jit(solution)/shard_map/pallas_call | solution.py:469
  46.7 0.0 copy-start.1
  46.7 0.0 copy-start
  46.7 1.1 %convert_bitcast_fusion = f32[27,2,4,8,128]{4,3,0,2,1:T(8,128)S(1)} fusion(bf16[2,4,28,8,128]{4,3,2,1,0:T(8,128)(2,1)} %bitcast.15), kind=kLoop, calls=%fused_computation | loop fusion | flops 221184 | bytes 1327104 | tf_op jit(solution)/shard_map/convert_element_type | solution.py:522
  47.8 1.0 %copy.7 = f32[27,2,4,8,128]{4,3,2,1,0:T(8,128)} copy(f32[27,2,4,8,128]{4,3,0,2,1:T(8,128)S(1)} %convert_bitcast_fusion) | data formatting | bytes 1769472 | tf_op jit(solution)/shard_map/convert_element_type | solution.py:522
  48.9 0.0 copy-done.1
  48.9 0.6 %copy.10 = bf16[1,64,2,256]{3,2,1,0:T(2,128)(2,1)} copy(bf16[1,64,2,256]{3,2,1,0:T(2,128)(2,1)S(1)} %bitcast.18) | data formatting | bytes 131072
  49.5 0.0 copy-done
  49.5 0.6 %copy.11 = f32[27,128,8]{1,2,0:T(8,128)} copy(f32[27,128,8]{1,2,0:T(8,128)S(1)} %bitcast.16) | data formatting | bytes 221184
Async XLA Ops:
  46.7 2.2 %copy-start.1 = (bf16[64,2,256]{2,1,0:T(2,128)(2,1)S(1)}, bf16[64,2,256]{2,1,0:T(2,128)(2,1)}, u32[]{:S(2)}) copy-start(bf16[64,2,256]{2,1,0:T(2,128)(2,1)} %get-tuple-element.6) | copy-start | bytes 196612
  46.7 2.8 %copy-start = (f32[27,8,128]{2,1,0:T(8,128)S(1)}, f32[27,8,128]{2,1,0:T(8,128)}, u32[]{:S(2)}) copy-start(f32[27,8,128]{2,1,0:T(8,128)} %get-tuple-element.8) | copy-start | bytes 331780

commit v5 on v4

--- a/solution.py
+++ b/solution.py
@@ -433,13 +433,23 @@
     wait_part(recv, A_OUT, aout.at[0, pl.ds(0, ny * NX - 1)])
     a_out_core = start(aout.at[c], aout.at[c], A_OUT_C, core)
 
+    def put_ga(core_part):
+        for n in range(ny):
+            rows = pl.ds(pl.multiple_of((core_part * ny + n) * rows_a, rows_a), rows_a)
+            for xx in range(NX):
+                some = min(taps_x, 27 - xx * taps_x)
+                part = aout[core_part, n * NX + xx, 0:some]
+                ga_ref[xx * taps_x : xx * taps_x + some, rows, :] = part.astype(F32)
+
+    put_ga(c)
+
     wait_part(recv, B_OUT, bag.at[pl.ds(0, nd - 1)])
     for tap in range(27):
         gb_ref[tap] = jnp.concatenate(
             [bag[e, :, tap * chans : (tap + 1) * chans].astype(F32) for e in range(nd)], axis=1
         )
     a_out_core.wait_recv()
-    ga_ref[...] = aout[...]
+    put_ga(1 - c)
 
     for copy in started:
         copy.wait_send()
@@ -470,7 +480,7 @@
         functools.partial(kernel, nd, ns, scale_a, scale_b),
         out_shape=(
             jax.ShapeDtypeStruct((64, 2, CELLS), BF16),
-            jax.ShapeDtypeStruct((NC, ny * NX) + block_a, BF16),
+            jax.ShapeDtypeStruct((27, 64, 128), F32),
             jax.ShapeDtypeStruct((27, filters, 128), F32),
         ),
         in_specs=[hbm] * 4,
@@ -518,9 +528,7 @@
         ],
         compiler_params=pltpu.CompilerParams(collective_id=0, has_side_effects=True),
     )(features[0], wa, wb, up)
-    ga = ga.reshape(NC, ny, NX * taps_x, rows_a, 128)[:, :, :27]
-    grad_a = jnp.transpose(ga, (2, 0, 1, 3, 4)).reshape(27, 64, 128).astype(F32)
-    return gi[None], grad_a, jnp.transpose(gb, (0, 2, 1))
+    return gi[None], ga, jnp.transpose(gb, (0, 2, 1))
 
 
 def solution(mesh):

time: 50.3 us -> 51.4 us (1.022)
  local copies, waits for them, and re-layouts: 2.31 us -> 4.37 us
  other arithmetic: 1.11 us -> 0 us
    unnamed x6 -> x5, local copies, waits for them, and re-layouts: 1.28 us -> 4.37 us
    convert_element_type x1 -> x0, other arithmetic: 1.11 us -> none  [body(): grad_a = jnp.transpose(ga, (2, 0, 1, 3, 4)).reshape(27, 64, 128).astype(F32)]
    convert_element_type x1 -> x0, local copies, waits for them, and re-layouts: 1.03 us -> none  [body(): grad_a = jnp.transpose(ga, (2, 0, 1, 3, 4)).reshape(27, 64, 128).astype(F32)]
where the time goes in v5:
time: 51.4 us; the launch traced here: 51.2 us
  Pallas kernels  46.2 us (90%)
  local copies, waits for them, and re-layouts  4.37 us (9%)
  between operations  0.65 us (1%)
    pallas_call x1, Pallas kernels, body(): pl.pallas_call(functools.partial(kernel, nd, ns, scale_a, scale_b), out_s...  46.2 us
    unnamed x5, local copies, waits for them, and re-layouts  4.37 us

profile of v5, /device:TPU:1, one launch (start us, length us, event | category | flops | bytes accessed | tf_op | source)
XLA Modules:
  0.0 51.2 jit_solution(10526583637710028841)
XLA Ops:
  0.6 46.2 %shard_map.67 = (bf16[64,2,256]{2,1,0:T(2,128)(2,1)}, f32[27,64,128]{2,1,0:T(8,128)}, f32[27,8,128]{2,1,0:T(8,128)}) custom-call(bf16[64,2,256]{2,1,0:T(2,128)(2,1)} %bitcast.11, bf16[9,192,128]{2,1,0:T(8,128)(2,1)} %bitcast.9, bf16[3,1152,256]{2,1,0:T(8,128)(2,1)} %bitcast.8, bf16[64,256]{1,0:T(8,128)(2,1)} %bitcast.13), custom_call_target="tpu_custom_call" | custom-call | tf_op jit(solution)/shard_map/pallas_call | solution.py:479
  46.8 0.0 copy-start
  46.8 1.5 %copy.10 = bf16[1,64,2,256]{3,2,1,0:T(2,128)(2,1)} copy(bf16[1,64,2,256]{3,2,1,0:T(2,128)(2,1)} %bitcast.12) | data formatting | bytes 131072
  48.4 2.2 %copy.11 = f32[27,64,128]{2,1,0:T(8,128)} copy(f32[27,64,128]{2,1,0:T(8,128)} %get-tuple-element.13) | data formatting | bytes 1769472
  50.6 0.0 copy-done
  50.6 0.6 %copy.12 = f32[27,128,8]{1,2,0:T(8,128)} copy(f32[27,128,8]{1,2,0:T(8,128)S(1)} %bitcast.10) | data formatting | bytes 221184
Async XLA Ops:
  46.8 3.7 %copy-start = (f32[27,8,128]{2,1,0:T(8,128)S(1)}, f32[27,8,128]{2,1,0:T(8,128)}, u32[]{:S(2)}) copy-start(f32[27,8,128]{2,1,0:T(8,128)} %get-tuple-element.8) | copy-start | bytes 331780
